TPU v7x, 256 devices: a whole 4x4x8 slice. The times are simulated.
256 devices in a mesh: graph: 32 (over z, y), feat: 8 (over x, core).
Axes of the slice: x: 4, y: 4, z: 8, core: 2. Of those that a mesh axis runs over, the one named last changes fastest.
Arguments:
- features: bfloat16 [65536, 1024], P('graph', 'feat'), may hold values from -6 to 6
- w_self: bfloat16 [1024, 1024], replicated, may hold values from -0.1875 to 0.1875
- w_neigh: bfloat16 [1024, 1024], replicated, may hold values from -0.1875 to 0.1875
- adjacency: bfloat16 [4096, 128, 128], P('graph'), may hold values from 0 to 1.5, as said below
- block_source: int32 [4096], P('graph'), may hold values from 0 to 15
- block_to_slot: int32 [4096], P('graph'), may hold values from 0 to 63
- send_rows: int32 [32, 32, 256], P('graph'), may hold values from 0 to 2047
- send_counts: int32 [32, 32], P('graph'), may hold values from 64 to 256, as said below
- degree: int32 [65536], P('graph'), may hold values from 8 to 32
- cotangent: bfloat16 [65536, 1024], P('graph', 'feat'), may hold values from -6 to 6
Outputs:
- hidden_out: bfloat16 [65536, 1024], P('graph', 'feat')
- grad_features: bfloat16 [65536, 1024], P('graph', 'feat')
- grad_self: float32 [1024, 1024], P('feat')
- grad_neigh: float32 [1024, 1024], P('feat')
Inputs may be any that keep to these rules, and one draw needn't show every extreme that they name: Slots 0 to send_counts[p, q] - 1 from p to q are live; in every draw some partition receives 256 live slots from every partition. `adjacency`: edge weights; a block is mostly zeros.
All inputs are finite; a program needn't handle non-finite values.
Results may differ from a plain program's by a relative error of at most 0.0066.
Values may be sent and summed in bfloat16 or wider, within the bound.
No kernel may reach another device: no remote copies, remote signals or barrier semaphores. Data moves between devices by JAX's collectives and lax.ppermute only.
A program may use at most 128 MiB of HBM per device.

v0:
```python
import jax
import jax.numpy as jnp
from jax import lax
from jax.sharding import PartitionSpec as P


def silu_slope(values):
    sig = jax.nn.sigmoid(values)
    return sig * (1.0 + values * (1.0 - sig))


def on_device(
    features,
    w_self,
    w_neigh,
    adjacency,
    block_source,
    block_to_slot,
    send_rows,
    send_counts,
    degree,
    cotangent,
):
    node_rows, feat_cols = features.shape
    part_count = lax.axis_size("graph")
    block_size = adjacency.shape[1]
    slot_cap = send_rows.shape[2]
    slot_total = part_count * slot_cap // block_size
    source_count = node_rows // block_size
    column_start = lax.axis_index("feat") * feat_cols
    sources = features.reshape(source_count, block_size, feat_cols)
    picked = jnp.take(sources, block_source, axis=0)
    prods = jnp.einsum("kij,kjd->kid", adjacency, picked, preferred_element_type=jnp.float32)
    slot_sums = jax.ops.segment_sum(prods, block_to_slot, num_segments=slot_total)
    live_counts = send_counts[0]
    is_live = jnp.arange(slot_cap, dtype=jnp.int32)[None, :] < live_counts[:, None]
    outgoing = jnp.where(
        is_live[:, :, None], slot_sums.reshape(part_count, slot_cap, feat_cols), 0.0
    ).astype(jnp.bfloat16)
    row_ids = jnp.where(is_live, send_rows[0], -1)
    incoming, incoming_ids = (
        lax.all_to_all(outgoing, "graph", split_axis=0, concat_axis=0, tiled=True),
        lax.all_to_all(row_ids, "graph", split_axis=0, concat_axis=0, tiled=True),
    )
    valid_slot = incoming_ids >= 0
    target_rows = jnp.where(valid_slot, incoming_ids, node_rows).reshape(-1)
    neighbor_sum = (
        jnp.zeros((node_rows, feat_cols), jnp.float32)
        .at[target_rows]
        .add(incoming.reshape(-1, feat_cols).astype(jnp.float32), mode="drop")
    )
    degrees = degree.astype(jnp.float32)[:, None]
    neighbor_mean = (neighbor_sum / degrees).astype(jnp.bfloat16)
    self_rows = lax.dynamic_slice_in_dim(w_self, column_start, feat_cols, 0)
    neigh_rows = lax.dynamic_slice_in_dim(w_neigh, column_start, feat_cols, 0)
    own_term = lax.dot_general(
        self_rows, features, (((0,), (1,)), ((), ())), preferred_element_type=jnp.float32
    )
    agg_term = lax.dot_general(
        neigh_rows, neighbor_mean, (((0,), (1,)), ((), ())), preferred_element_type=jnp.float32
    )
    pre_act = lax.psum_scatter(own_term + agg_term, "feat", scatter_dimension=0, tiled=True).T
    hidden_out = jax.nn.silu(pre_act).astype(jnp.bfloat16)
    grad_pre = (cotangent.astype(jnp.float32) * silu_slope(pre_act)).astype(jnp.bfloat16)
    grad_full = lax.all_gather(grad_pre, "feat", axis=1, tiled=True)
    local_self = lax.dot_general(
        features, grad_full, (((0,), (0,)), ((), ())), preferred_element_type=jnp.float32
    )
    local_neigh = lax.dot_general(
        neighbor_mean, grad_full, (((0,), (0,)), ((), ())), preferred_element_type=jnp.float32
    )
    grad_self, grad_neigh = lax.psum((local_self, local_neigh), "graph")
    self_grad = lax.dot_general(
        grad_full, self_rows, (((1,), (1,)), ((), ())), preferred_element_type=jnp.float32
    )
    back_rows = (
        lax.dot_general(
            grad_full, neigh_rows, (((1,), (1,)), ((), ())), preferred_element_type=jnp.float32
        )
        / degrees
    ).astype(jnp.bfloat16)
    lookup = jnp.where(valid_slot, incoming_ids, 0)
    sending_back = jnp.where(valid_slot[:, :, None], jnp.take(back_rows, lookup, axis=0), 0.0)
    returned = lax.all_to_all(sending_back, "graph", split_axis=0, concat_axis=0, tiled=True)
    slot_blocks = returned.reshape(slot_total, block_size, feat_cols)
    chosen = jnp.take(slot_blocks, block_to_slot, axis=0)
    contrib = jnp.einsum("kij,kid->kjd", adjacency, chosen, preferred_element_type=jnp.float32)
    neigh_grad = jax.ops.segment_sum(contrib, block_source, num_segments=source_count).reshape(
        node_rows, feat_cols
    )
    grad_features = (self_grad + neigh_grad).astype(jnp.bfloat16)
    return (hidden_out, grad_features, grad_self, grad_neigh)


def solution(mesh):
    placed = (
        P("graph", "feat"),
        P(),
        P(),
        P("graph", None, None),
        P("graph"),
        P("graph"),
        P("graph", None, None),
        P("graph", None),
        P("graph"),
        P("graph", "feat"),
    )
    return jax.shard_map(
        on_device,
        mesh=mesh,
        in_specs=placed,
        out_specs=(P("graph", "feat"), P("graph", "feat"), P("feat", None), P("feat", None)),
        check_vma=False,
    )
```

profile of v0, /device:TPU:2, one launch (start us, length us, event | category | flops | bytes accessed | tf_op | source)
XLA Modules:
  0.0 545.4 jit_solution(14531779473950020415)
XLA Ops:
  8.8 11.5 %all-to-all-start = ((s32[32,1,256]{2,1,0:T(1,128)}), s32[32,1,256]{2,1,0:T(1,128)S(1)}, u32[]{:S(2)}, u32[]{:S(2)}) async-start(s32[32,1,256]{2,1,0:T(1,128)} %compare_select_fusion.4), calls=%async_computation | async-start | bytes 65536 | tf_op jit(solution)/shard_map/all_to_all | solution.py:43
  22.4 4.1 gather_fusion
  26.4 9.9 %fusion.9 = f32[128,128,128]{1,2,0:T(8,128)} fusion(bf16[128,128,128]{2,1,0:T(8,128)(2,1)} %param.13, bf16[128,128,128]{2,1,0:T(8,128)(2,1)} %gather_fusion, pred[128]{0:T(512)(128)(4,1)S(1)} %compare_and_fusion.2), kind=kOutput, calls=%fused_computation.17 | convolution fusion | flops 538968064 | bytes 16777344 | tf_op jit(solution)/shard_map/kij,kjd->kid/dot_general | solution.py:33
  36.4 9.0 %copy.27 = f32[128,128,128]{2,1,0:T(8,128)} copy(f32[128,128,128]{1,2,0:T(8,128)} %fusion.9) | data formatting | bytes 16777216 | tf_op jit(solution)/shard_map/kij,kjd->kid/dot_general | solution.py:33
  47.9 26.8 %scatter_fusion = f32[64,128,128]{2,1,0:T(8,128)} fusion(f32[64,128,128]{2,1,0:T(8,128)} %broadcast_in_dim.92, s32[128]{0:T(128)S(1)} %copy-done.8, f32[128,128,128]{2,1,0:T(8,128)} %copy.27), kind=kCustom, calls=%fused_computation.3 | custom fusion | flops 2097152 | bytes 25166336 | tf_op jit(solution)/shard_map/scatter-add | solution.py:34
  74.7 4.9 fusion.2
  79.6 9.7 %all-to-all-start.1 = ((bf16[32,256,128]{2,1,0:T(8,128)(2,1)}), bf16[32,256,128]{2,1,0:T(8,128)(2,1)}, u32[]{:S(2)}, u32[]{:S(2)}) async-start(bf16[32,256,128]{2,1,0:T(8,128)(2,1)} %fusion.2), calls=%async_computation.1 | async-start | bytes 4194304 | tf_op jit(solution)/shard_map/all_to_all | solution.py:42
  89.4 5.5 %fusion.31 = f32[1024,2048]{1,0:T(8,128)} fusion(bf16[2048,128]{1,0:T(8,128)(2,1)S(1)} %copy-done.2, bf16[1024,1024]{1,0:T(8,128)(2,1)} %param.11, s32[]{:T(128)S(6)} %select_n.95), kind=kOutput, calls=%fused_computation.43 | convolution fusion | flops 536870912 | bytes 9175044 | tf_op jit(solution)/shard_map/dot_general | solution.py:56
  94.9 44.0 %all-to-all-done.1 = bf16[32,256,128]{2,1,0:T(8,128)(2,1)} async-done(((bf16[32,256,128]{2,1,0:T(8,128)(2,1)}), bf16[32,256,128]{2,1,0:T(8,128)(2,1)}, u32[]{:S(2)}, u32[]{:S(2)}) %all-to-all-start.1) | async-done | bytes 2097184 | tf_op jit(solution)/shard_map/all_to_all | solution.py:42
  138.8 45.6 %scatter_custom_fusion.1 = f32[2048,128]{1,0:T(8,128)} fusion(s32[8192]{0:T(1024)S(1)} %bitcast.71, bf16[8192,128]{1,0:T(8,128)(2,1)} %bitcast.15, f32[]{:T(128)} %constant.32.clone.1), kind=kCustom, calls=%fused_computation.7 | custom fusion | flops 2097152 | bytes 3145732 | tf_op jit(solution)/shard_map/scatter-add | solution.py:50
  184.4 8.3 %convolution_add_fusion = f32[1024,2048]{1,0:T(8,128)} fusion(f32[1024,2048]{1,0:T(8,128)} %fusion.31, bf16[1024,1024]{1,0:T(8,128)(2,1)S(1)} %copy-done, s32[]{:T(128)S(6)} %select_n.95, f32[2048,128]{1,0:T(8,128)} %scatter_custom_fusion.1, f32[2048]{0:T(1024)S(1)} %convert_element_type.35), kind=kOutput, calls=%fused_computation.6 | convolution fusion | flops 539492352 | bytes 18096132 | tf_op jit(solution)/shard_map/dot_general | solution.py:59
  194.2 48.7 %reduce-scatter.2.cloned.1.call-done = f32[128,2048]{1,0:T(8,128)} async-done(((f32[1024,2048]{1,0:T(8,128)}), f32[128,2048]{1,0:T(8,128)}) %reduce-scatter.2.cloned.1.call-update) | async-done | bytes 1048592 | tf_op jit(solution)/shard_map/reduce_scatter | solution.py:62
  245.7 35.7 %all-gather.2.cloned.1.call-done = bf16[2048,1024]{0,1:T(8,128)(2,1)} async-done(((bf16[2048,128]{0,1:T(8,128)(2,1)}), bf16[2048,1024]{0,1:T(8,128)(2,1)}) %all-gather.2.cloned.1.call-update) | async-done | bytes 4194320 | tf_op jit(solution)/shard_map/all_gather | solution.py:65
  281.4 3.6 fusion.16
  285.0 24.0 %gather_fusion.1 = bf16[8192,128]{1,0:T(8,128)(2,1)S(1)} fusion(bf16[2048,128]{1,0:T(8,128)(2,1)S(1)} %fusion.16, s32[8192]{0:T(1024)S(1)} %broadcast_clamp_fusion), kind=kCustom, calls=%fused_computation.1 | custom fusion | bytes 4227072 | tf_op jit(solution)/shard_map/jit(_take)/gather | solution.py:83
  309.0 4.6 select_select_fusion
  313.7 9.9 %all-to-all-start.2 = ((bf16[32,256,128]{2,1,0:T(8,128)(2,1)}), bf16[32,256,128]{2,1,0:T(8,128)(2,1)S(1)}, u32[]{:S(2)}, u32[]{:S(2)}) async-start(bf16[32,256,128]{2,1,0:T(8,128)(2,1)} %select_select_fusion), calls=%async_computation.3 | async-start | bytes 4194304 | tf_op jit(solution)/shard_map/all_to_all | solution.py:84
  323.6 4.4 convolution_bitcast_fusion
  331.9 162.1 %all-reduce.3.cloned.1.call-done = (f32[128,1024]{0,1:T(8,128)}, f32[128,1024]{1,0:T(8,128)}) async-done(((f32[128,1024]{0,1:T(8,128)}, f32[128,1024]{1,0:T(8,128)}), (f32[128,1024]{0,1:T(8,128)}, f32[128,1024]{1,0:T(8,128)})) %all-reduce.3.cloned.1.call-update) | async-done | bytes 1048592 | tf_op jit(solution)/shard_map/psum | solution.py:72
  496.0 3.0 gather_fusion.2
  499.0 8.4 %fusion.12 = f32[128,128,128]{1,2,0:T(8,128)} fusion(bf16[128,128,128]{2,1,0:T(8,128)(2,1)} %param.13, bf16[128,128,128]{2,1,0:T(8,128)(2,1)} %gather_fusion.2, pred[128]{0:T(512)(128)(4,1)S(1)} %compare_and_fusion.1), kind=kOutput, calls=%fused_computation.18 | convolution fusion | flops 538968064 | bytes 16777344 | tf_op jit(solution)/shard_map/kij,kid->kjd/dot_general | solution.py:87
  507.4 9.0 %copy.30 = f32[128,128,128]{2,1,0:T(8,128)} copy(f32[128,128,128]{1,2,0:T(8,128)} %fusion.12) | data formatting | bytes 16777216 | tf_op jit(solution)/shard_map/kij,kid->kjd/dot_general | solution.py:87
  516.5 17.0 %scatter_fusion.1 = f32[16,128,128]{2,1,0:T(8,128)S(1)} fusion(f32[16,128,128]{2,1,0:T(8,128)S(1)} %broadcast_in_dim.98, s32[128]{0:T(128)S(1)} %copy-done.9, f32[128,128,128]{2,1,0:T(8,128)} %copy.30), kind=kCustom, calls=%fused_computation.5 | custom fusion | flops 2097152 | bytes 25166336 | tf_op jit(solution)/shard_map/scatter-add | solution.py:88
  533.6 4.5 fusion.15
  (49 shorter events, 17.3 us)
Async XLA Ops:
  7.2 177.2 %copy-start = (bf16[1024,1024]{1,0:T(8,128)(2,1)S(1)}, bf16[1024,1024]{1,0:T(8,128)(2,1)}, u32[]{:S(2)}) copy-start(bf16[1024,1024]{1,0:T(8,128)(2,1)} %param.12) | copy-start | bytes 6291460
  8.8 70.8 %all-to-all-start = ((s32[32,1,256]{2,1,0:T(1,128)}), s32[32,1,256]{2,1,0:T(1,128)S(1)}, u32[]{:S(2)}, u32[]{:S(2)}) async-start(s32[32,1,256]{2,1,0:T(1,128)} %compare_select_fusion.4), calls=%async_computation | async-start | bytes 65536 | tf_op jit(solution)/shard_map/all_to_all | solution.py:43
  45.4 2.5 copy-start.8
  74.7 14.6 %copy-start.7 = (s32[2048]{0:T(1024)S(1)}, s32[2048]{0:T(1024)}, u32[]{:S(2)}) copy-start(s32[2048]{0:T(1024)} %param.18) | copy-start | bytes 24580
  74.7 14.6 %copy-start.2 = (bf16[2048,128]{1,0:T(8,128)(2,1)S(1)}, bf16[2048,128]{1,0:T(8,128)(2,1)}, u32[]{:S(2)}) copy-start(bf16[2048,128]{1,0:T(8,128)(2,1)} %param.10) | copy-start | bytes 1572868
  79.6 59.3 %all-to-all-start.1 = ((bf16[32,256,128]{2,1,0:T(8,128)(2,1)}), bf16[32,256,128]{2,1,0:T(8,128)(2,1)}, u32[]{:S(2)}, u32[]{:S(2)}) async-start(bf16[32,256,128]{2,1,0:T(8,128)(2,1)} %fusion.2), calls=%async_computation.1 | async-start | bytes 4194304 | tf_op jit(solution)/shard_map/all_to_all | solution.py:42
  89.3 153.6 %reduce-scatter.2.cloned.1.call-start = ((), (), s32[]{:S(2)}) async-start(), calls=%async_computation.4 | async-start | bytes 9437184 | tf_op jit(solution)/shard_map/reduce_scatter | solution.py:62
  192.8 88.6 %all-gather.2.cloned.1.call-start = ((), (), s32[]{:S(2)}) async-start(), calls=%async_computation.5 | async-start | bytes 4718592 | tf_op jit(solution)/shard_map/all_gather | solution.py:65
  313.7 182.3 %all-to-all-start.2 = ((bf16[32,256,128]{2,1,0:T(8,128)(2,1)}), bf16[32,256,128]{2,1,0:T(8,128)(2,1)S(1)}, u32[]{:S(2)}, u32[]{:S(2)}) async-start(bf16[32,256,128]{2,1,0:T(8,128)(2,1)} %select_select_fusion), calls=%async_computation.3 | async-start | bytes 4194304 | tf_op jit(solution)/shard_map/all_to_all | solution.py:84
  323.5 170.4 %all-reduce.3.cloned.1.call-start = ((), (), s32[]{:S(2)}) async-start(), calls=%async_computation.6 | async-start | bytes 2097152 | tf_op jit(solution)/shard_map/psum | solution.py:72
  323.6 4.4 copy-start.3
  323.6 4.4 copy-start.4
  328.0 2.9 copy-start.5
  507.4 9.1 %copy-start.9 = (s32[128]{0:T(128)S(1)}, s32[128]{0:T(128)}, u32[]{:S(2)}) copy-start(s32[128]{0:T(128)} %param.14) | copy-start | bytes 1540
  533.6 4.5 copy-start.6
  533.6 5.3 copy-start.1
Sparse Core Ops, SparseCore 0:
  192.9 49.9 reduce-scatter.1
  245.7 35.6 all-gather.1
  330.9 162.9 all-reduce.2
where the time goes:
time: 547 us; the launch traced here: 545 us
  waiting for transfers between devices  290 us (53%)
  other arithmetic  105 us (19%)
  local copies, waits for them, and re-layouts  56.8 us (10%)
  matrix products  47.4 us (9%)
  starting transfers between devices  31.3 us (6%)
  between operations  14 us (3%)
    psum x1, waiting for transfers between devices, on_device(): grad_self, grad_neigh = lax.psum((local_self, local_neigh), 'graph')  162 us
    reduce_scatter x1, waiting for transfers between devices, on_device(): lax.psum_scatter(own_term + agg_term, 'feat', scatter_dimension=0, tiled=...  48.7 us
    scatter-add x1, other arithmetic, on_device(): neighbor_sum = jnp.zeros((node_rows, feat_cols), jnp.float32).at[target_r...  45.6 us
    all_to_all x1, waiting for transfers between devices, on_device(): lax.all_to_all(outgoing, 'graph', split_axis=0, concat_axis=0, tiled=True)  44 us
    all_gather x1, waiting for transfers between devices, on_device(): grad_full = lax.all_gather(grad_pre, 'feat', axis=1, tiled=True)  35.7 us
    scatter-add x1, other arithmetic, on_device(): jax.ops.segment_sum(prods, block_to_slot, num_segments=slot_total)  26.8 us
    gather x1, local copies, waits for them, and re-layouts, on_device(): jnp.take(back_rows, lookup, axis=0)  24 us
    scatter-add x1, other arithmetic, on_device(): jax.ops.segment_sum(contrib, block_source, num_segments=source_count)  17 us
  transfers between devices with their start and end apart: 6, of which 4 were waited for; matrix products, arithmetic and copies ran while one was open for 14% of the time, Pallas kernels for 0%

commit v1 on v0

--- a/solution.py
+++ b/solution.py
@@ -62,7 +62,9 @@
     pre_act = lax.psum_scatter(own_term + agg_term, "feat", scatter_dimension=0, tiled=True).T
     hidden_out = jax.nn.silu(pre_act).astype(jnp.bfloat16)
     grad_pre = (cotangent.astype(jnp.float32) * silu_slope(pre_act)).astype(jnp.bfloat16)
-    grad_full = lax.all_gather(grad_pre, "feat", axis=1, tiled=True)
+    grad_full = jnp.concatenate(
+        lax.all_to_all(jnp.stack([grad_pre] * lax.axis_size("feat")), "feat", 0, 0), axis=1
+    )
     local_self = lax.dot_general(
         features, grad_full, (((0,), (0,)), ((), ())), preferred_element_type=jnp.float32
     )

time: 547 us -> 569 us (1.040)
  waiting for transfers between devices: 290 us -> 301 us
  starting transfers between devices: 31.3 us -> 38.7 us
    all_to_all x0 -> x1, waiting for transfers between devices: none -> 48.2 us  [on_device(): lax.all_to_all(jnp.stack([grad_pre] * lax.axis_size('feat')), 'feat', 0, 0)]
    all_gather x1 -> x0, waiting for transfers between devices: 35.7 us -> none  [on_device(): grad_full = lax.all_gather(grad_pre, 'feat', axis=1, tiled=True)]
    all_to_all x0 -> x1, starting transfers between devices: none -> 7.37 us  [on_device(): lax.all_to_all(jnp.stack([grad_pre] * lax.axis_size('feat')), 'feat', 0, 0)]
where the time goes in v1:
time: 569 us; the launch traced here: 567 us
  waiting for transfers between devices  301 us (53%)
  other arithmetic  105 us (18%)
  local copies, waits for them, and re-layouts  59.3 us (10%)
  matrix products  49.5 us (9%)
  starting transfers between devices  38.7 us (7%)
  between operations  14.2 us (2%)
    psum x1, waiting for transfers between devices, on_device(): grad_self, grad_neigh = lax.psum((local_self, local_neigh), 'graph')  159 us
    reduce_scatter x1, waiting for transfers between devices, on_device(): lax.psum_scatter(own_term + agg_term, 'feat', scatter_dimension=0, tiled=...  48.9 us
    all_to_all x1, waiting for transfers between devices, on_device(): lax.all_to_all(jnp.stack([grad_pre] * lax.axis_size('feat')), 'feat', 0, 0)  48.2 us
    scatter-add x1, other arithmetic, on_device(): neighbor_sum = jnp.zeros((node_rows, feat_cols), jnp.float32).at[target_r...  45.6 us
    all_to_all x1, waiting for transfers between devices, on_device(): lax.all_to_all(outgoing, 'graph', split_axis=0, concat_axis=0, tiled=True)  44 us
    scatter-add x1, other arithmetic, on_device(): jax.ops.segment_sum(prods, block_to_slot, num_segments=slot_total)  26.7 us
    gather x1, local copies, waits for them, and re-layouts, on_device(): jnp.take(back_rows, lookup, axis=0)  24 us
    scatter-add x1, other arithmetic, on_device(): jax.ops.segment_sum(contrib, block_source, num_segments=source_count)  17 us
  transfers between devices with their start and end apart: 6, of which 4 were waited for; matrix products, arithmetic and copies ran while one was open for 14% of the time, Pallas kernels for 0%

profile of v1, /device:TPU:2, one launch (start us, length us, event | category | flops | bytes accessed | tf_op | source)
XLA Modules:
  0.0 567.5 jit_solution(11346938930478799305)
XLA Ops:
  8.8 11.5 %all-to-all-start = ((s32[32,1,256]{2,1,0:T(1,128)}), s32[32,1,256]{2,1,0:T(1,128)S(1)}, u32[]{:S(2)}, u32[]{:S(2)}) async-start(s32[32,1,256]{2,1,0:T(1,128)} %compare_select_fusion.4), calls=%async_computation | async-start | bytes 65536 | tf_op jit(solution)/shard_map/all_to_all | solution.py:43
  22.4 4.1 gather_fusion
  26.4 9.9 %fusion.9 = f32[128,128,128]{1,2,0:T(8,128)} fusion(bf16[128,128,128]{2,1,0:T(8,128)(2,1)} %param.13, bf16[128,128,128]{2,1,0:T(8,128)(2,1)} %gather_fusion, pred[128]{0:T(512)(128)(4,1)S(1)} %compare_and_fusion.2), kind=kOutput, calls=%fused_computation.17 | convolution fusion | flops 538968064 | bytes 16777344 | tf_op jit(solution)/shard_map/kij,kjd->kid/dot_general | solution.py:33
  36.4 9.0 %copy.28 = f32[128,128,128]{2,1,0:T(8,128)} copy(f32[128,128,128]{1,2,0:T(8,128)} %fusion.9) | data formatting | bytes 16777216 | tf_op jit(solution)/shard_map/kij,kjd->kid/dot_general | solution.py:33
  47.8 26.7 %scatter_fusion = f32[64,128,128]{2,1,0:T(8,128)} fusion(f32[64,128,128]{2,1,0:T(8,128)} %broadcast_in_dim.92, s32[128]{0:T(128)S(1)} %copy-done.7, f32[128,128,128]{2,1,0:T(8,128)} %copy.28), kind=kCustom, calls=%fused_computation.3 | custom fusion | flops 2097152 | bytes 25166336 | tf_op jit(solution)/shard_map/scatter-add | solution.py:34
  74.5 4.9 fusion.2
  79.4 9.9 %all-to-all-start.1 = ((bf16[32,256,128]{2,1,0:T(8,128)(2,1)}), bf16[32,256,128]{2,1,0:T(8,128)(2,1)}, u32[]{:S(2)}, u32[]{:S(2)}) async-start(bf16[32,256,128]{2,1,0:T(8,128)(2,1)} %fusion.2), calls=%async_computation.1 | async-start | bytes 4194304 | tf_op jit(solution)/shard_map/all_to_all | solution.py:42
  89.4 5.5 fusion.31
  94.9 44.0 %all-to-all-done.1 = bf16[32,256,128]{2,1,0:T(8,128)(2,1)} async-done(((bf16[32,256,128]{2,1,0:T(8,128)(2,1)}), bf16[32,256,128]{2,1,0:T(8,128)(2,1)}, u32[]{:S(2)}, u32[]{:S(2)}) %all-to-all-start.1) | async-done | bytes 2097184 | tf_op jit(solution)/shard_map/all_to_all | solution.py:42
  138.9 45.6 %scatter_custom_fusion.1 = f32[2048,128]{1,0:T(8,128)} fusion(s32[8192]{0:T(1024)S(1)} %bitcast.74, bf16[8192,128]{1,0:T(8,128)(2,1)} %bitcast.18, f32[]{:T(128)} %constant.32.clone.1), kind=kCustom, calls=%fused_computation.7 | custom fusion | flops 2097152 | bytes 3145732 | tf_op jit(solution)/shard_map/scatter-add | solution.py:50
  184.4 8.3 %convolution_add_fusion = f32[1024,2048]{1,0:T(8,128)} fusion(f32[1024,2048]{1,0:T(8,128)} %fusion.31, bf16[1024,1024]{1,0:T(8,128)(2,1)S(1)} %copy-done, s32[]{:T(128)S(6)} %select_n.95, f32[2048,128]{1,0:T(8,128)} %scatter_custom_fusion.1, f32[2048]{0:T(1024)S(1)} %convert_element_type.35), kind=kOutput, calls=%fused_computation.6 | convolution fusion | flops 539492352 | bytes 18096132 | tf_op jit(solution)/shard_map/dot_general | solution.py:59
  194.0 48.9 %reduce-scatter.2.cloned.1.call-done = f32[128,2048]{1,0:T(8,128)} async-done(((f32[1024,2048]{1,0:T(8,128)}), f32[128,2048]{1,0:T(8,128)}) %reduce-scatter.2.cloned.1.call-update) | async-done | bytes 1048592 | tf_op jit(solution)/shard_map/reduce_scatter | solution.py:62
  247.9 7.4 %all-to-all-start.2 = ((bf16[8,2048,128]{1,2,0:T(8,128)(2,1)}), bf16[8,2048,128]{1,2,0:T(8,128)(2,1)}, u32[]{:S(2)}, u32[]{:S(2)}) async-start(bf16[8,2048,128]{1,2,0:T(8,128)(2,1)} %stack.2), calls=%async_computation.3 | async-start | bytes 8388608 | tf_op jit(solution)/shard_map/all_to_all | solution.py:66
  255.3 48.2 %all-to-all-done.2 = bf16[8,2048,128]{1,2,0:T(8,128)(2,1)} async-done(((bf16[8,2048,128]{1,2,0:T(8,128)(2,1)}), bf16[8,2048,128]{1,2,0:T(8,128)(2,1)}, u32[]{:S(2)}, u32[]{:S(2)}) %all-to-all-start.2) | async-done | bytes 4194336 | tf_op jit(solution)/shard_map/all_to_all | solution.py:66
  307.2 24.0 %gather_fusion.1 = bf16[8192,128]{1,0:T(8,128)(2,1)S(1)} fusion(bf16[2048,128]{1,0:T(8,128)(2,1)S(1)} %fusion.16, s32[8192]{0:T(1024)S(1)} %broadcast_clamp_fusion), kind=kCustom, calls=%fused_computation.1 | custom fusion | bytes 4227072 | tf_op jit(solution)/shard_map/jit(_take)/gather | solution.py:85
  331.3 4.6 select_select_fusion
  335.9 9.9 %all-to-all-start.3 = ((bf16[32,256,128]{2,1,0:T(8,128)(2,1)}), bf16[32,256,128]{2,1,0:T(8,128)(2,1)S(1)}, u32[]{:S(2)}, u32[]{:S(2)}) async-start(bf16[32,256,128]{2,1,0:T(8,128)(2,1)} %select_select_fusion), calls=%async_computation.4 | async-start | bytes 4194304 | tf_op jit(solution)/shard_map/all_to_all | solution.py:86
  345.8 4.3 convolution_bitcast_fusion
  350.1 5.1 fusion.39
  356.3 159.5 %all-reduce.3.cloned.1.call-done = (f32[128,1024]{0,1:T(8,128)}, f32[128,1024]{1,0:T(8,128)}) async-done(((f32[128,1024]{0,1:T(8,128)}, f32[128,1024]{1,0:T(8,128)}), (f32[128,1024]{0,1:T(8,128)}, f32[128,1024]{1,0:T(8,128)})) %all-reduce.3.cloned.1.call-update) | async-done | bytes 1048592 | tf_op jit(solution)/shard_map/psum | solution.py:74
  520.8 8.4 %fusion.12 = f32[128,128,128]{1,2,0:T(8,128)} fusion(bf16[128,128,128]{2,1,0:T(8,128)(2,1)} %param.13, bf16[128,128,128]{2,1,0:T(8,128)(2,1)} %gather_fusion.2, pred[128]{0:T(512)(128)(4,1)S(1)} %compare_and_fusion.1), kind=kOutput, calls=%fused_computation.18 | convolution fusion | flops 538968064 | bytes 16777344 | tf_op jit(solution)/shard_map/kij,kid->kjd/dot_general | solution.py:89
  529.2 9.0 %copy.31 = f32[128,128,128]{2,1,0:T(8,128)} copy(f32[128,128,128]{1,2,0:T(8,128)} %fusion.12) | data formatting | bytes 16777216 | tf_op jit(solution)/shard_map/kij,kid->kjd/dot_general | solution.py:89
  538.3 17.0 %scatter_fusion.1 = f32[16,128,128]{2,1,0:T(8,128)S(1)} fusion(f32[16,128,128]{2,1,0:T(8,128)S(1)} %broadcast_in_dim.98, s32[128]{0:T(128)S(1)} %copy-done.8, f32[128,128,128]{2,1,0:T(8,128)} %copy.31), kind=kCustom, calls=%fused_computation.5 | custom fusion | flops 2097152 | bytes 25166336 | tf_op jit(solution)/shard_map/scatter-add | solution.py:90
  555.4 4.5 fusion.15
  (47 shorter events, 23.3 us)
Async XLA Ops:
  7.2 177.3 %copy-start = (bf16[1024,1024]{1,0:T(8,128)(2,1)S(1)}, bf16[1024,1024]{1,0:T(8,128)(2,1)}, u32[]{:S(2)}) copy-start(bf16[1024,1024]{1,0:T(8,128)(2,1)} %param.12) | copy-start | bytes 6291460
  8.8 70.6 %all-to-all-start = ((s32[32,1,256]{2,1,0:T(1,128)}), s32[32,1,256]{2,1,0:T(1,128)S(1)}, u32[]{:S(2)}, u32[]{:S(2)}) async-start(s32[32,1,256]{2,1,0:T(1,128)} %compare_select_fusion.4), calls=%async_computation | async-start | bytes 65536 | tf_op jit(solution)/shard_map/all_to_all | solution.py:43
  45.4 2.5 copy-start.7
  74.5 14.8 %copy-start.6 = (s32[2048]{0:T(1024)S(1)}, s32[2048]{0:T(1024)}, u32[]{:S(2)}) copy-start(s32[2048]{0:T(1024)} %param.18) | copy-start | bytes 24580
  74.5 14.8 %copy-start.2 = (bf16[2048,128]{1,0:T(8,128)(2,1)S(1)}, bf16[2048,128]{1,0:T(8,128)(2,1)}, u32[]{:S(2)}) copy-start(bf16[2048,128]{1,0:T(8,128)(2,1)} %param.10) | copy-start | bytes 1572868
  79.4 59.5 %all-to-all-start.1 = ((bf16[32,256,128]{2,1,0:T(8,128)(2,1)}), bf16[32,256,128]{2,1,0:T(8,128)(2,1)}, u32[]{:S(2)}, u32[]{:S(2)}) async-start(bf16[32,256,128]{2,1,0:T(8,128)(2,1)} %fusion.2), calls=%async_computation.1 | async-start | bytes 4194304 | tf_op jit(solution)/shard_map/all_to_all | solution.py:42
  89.3 153.6 %reduce-scatter.2.cloned.1.call-start = ((), (), s32[]{:S(2)}) async-start(), calls=%async_computation.5 | async-start | bytes 9437184 | tf_op jit(solution)/shard_map/reduce_scatter | solution.py:62
  247.9 55.7 %all-to-all-start.2 = ((bf16[8,2048,128]{1,2,0:T(8,128)(2,1)}), bf16[8,2048,128]{1,2,0:T(8,128)(2,1)}, u32[]{:S(2)}, u32[]{:S(2)}) async-start(bf16[8,2048,128]{1,2,0:T(8,128)(2,1)} %stack.2), calls=%async_computation.3 | async-start | bytes 8388608 | tf_op jit(solution)/shard_map/all_to_all | solution.py:66
  335.9 181.9 %all-to-all-start.3 = ((bf16[32,256,128]{2,1,0:T(8,128)(2,1)}), bf16[32,256,128]{2,1,0:T(8,128)(2,1)S(1)}, u32[]{:S(2)}, u32[]{:S(2)}) async-start(bf16[32,256,128]{2,1,0:T(8,128)(2,1)} %select_select_fusion), calls=%async_computation.4 | async-start | bytes 4194304 | tf_op jit(solution)/shard_map/all_to_all | solution.py:86
  345.8 170.0 %all-reduce.3.cloned.1.call-start = ((), (), s32[]{:S(2)}) async-start(), calls=%async_computation.6 | async-start | bytes 2097152 | tf_op jit(solution)/shard_map/psum | solution.py:74
  345.8 4.3 copy-start.3
  350.1 5.1 copy-start.4
  529.2 9.1 %copy-start.8 = (s32[128]{0:T(128)S(1)}, s32[128]{0:T(128)}, u32[]{:S(2)}) copy-start(s32[128]{0:T(128)} %param.14) | copy-start | bytes 1540
  555.3 4.5 copy-start.5
  555.4 5.3 copy-start.1
Sparse Core Ops, SparseCore 0:
  192.9 49.9 reduce-scatter.1
  355.3 160.3 all-reduce.2
